TPU v7x, 256 devices: a whole 4x4x8 slice. The times are simulated.
256 devices in a mesh: dom: 32 (over x, z), grp: 8 (over y, core).
Axes of the slice: x: 4, y: 4, z: 8, core: 2. Of those that a mesh axis runs over, the one named last changes fastest.
Arguments:
- node_feats: bfloat16 [65536, 1024], P(('dom', 'grp')), may hold values from -6 to 6
- weight: bfloat16 [1024, 512], replicated, may hold values from -0.1875 to 0.1875
- bias: float32 [512], replicated, may hold values from -4 to 4
- cotangent: bfloat16 [65536, 512], P(('dom', 'grp')), may hold values from -6 to 6
- tile_bank: bfloat16 [16, 128, 128], replicated, may hold values from -0.125 to 0.125
- local_cols: int32 [32, 16, 16], P('dom'), may hold values from 0 to 15
- local_banks: int32 [32, 16, 16], P('dom'), may hold values from 0 to 15
- published: int32 [32, 4], P('dom'), may hold values from 0 to 15, as said below
- send_table: int32 [32, 32, 2], replicated, may hold values from -1 to 3, as said below
- halo_rows: int32 [32, 32, 2], P('dom'), may hold values from 0 to 15
- halo_banks: int32 [32, 32, 2], P('dom'), may hold values from 0 to 15
Outputs:
- activations: bfloat16 [65536, 512], P(('dom', 'grp'))
- grad_nodes: bfloat16 [65536, 1024], P(('dom', 'grp'))
- grad_weight: float32 [1024, 512], replicated
- grad_bias: float32 [512], replicated
Inputs may be any that keep to these rules, and one draw needn't show every extreme that they name: `published`: the 4 entries of a partition are distinct block numbers of that partition; 0 and 15 each appear in some partition's list. `send_table`: entry s of the pair (src, p) is -1 or an index into the offered list of src; the live entries of a pair come first and are distinct; a pair (p, p) has none; some pair has all 2 entries live.
All inputs are finite; a program needn't handle non-finite values.
Results may differ from a plain program's by a relative error of at most 0.019.
The roundings to bfloat16 on the way count: a program that leaves them out, or rounds other values in their place, can miss the bound.
Values may be sent and summed in bfloat16 or wider, within the bound.
A program may use at most 64 MiB of HBM per device.

v0:
```python
import jax
import jax.numpy as jnp
from jax import lax
from jax.sharding import PartitionSpec as P


def per_device(
    node_feats,
    weight,
    bias,
    cotangent,
    tile_bank,
    local_cols,
    local_banks,
    published,
    send_table,
    halo_rows,
    halo_banks,
):
    domains = lax.axis_size("dom")
    groups = lax.axis_size("grp")
    domain_index = lax.axis_index("dom")
    rows_here = node_feats.shape[0]
    tile_size = tile_bank.shape[1]
    slot_count = send_table.shape[2]
    pub_count = published.shape[1]
    tiles_row = local_cols.shape[2]
    features = lax.all_to_all(node_feats, "grp", split_axis=1, concat_axis=0, tiled=True)
    part_rows, narrow = features.shape
    blocks = part_rows // tile_size
    feat_blocks = features.reshape(blocks, tile_size, narrow)
    cols_here = local_cols[0]
    banks_here = local_banks[0]
    own_pub = published[0]
    incoming = lax.dynamic_index_in_dim(send_table, domain_index, 1, keepdims=False)
    live_in = (incoming >= 0).astype(jnp.float32)[:, :, None, None]
    rows_in = halo_rows[0]
    halo_tiles = tile_bank[halo_banks[0]]
    source_ids = lax.broadcasted_iota(jnp.int32, (domains, slot_count), 0)
    gathered_ids = source_ids * pub_count + jnp.maximum(incoming, 0)

    def forward_tiles(position, running):
        column = lax.dynamic_index_in_dim(cols_here, position, 1, keepdims=False)
        bank_ids = lax.dynamic_index_in_dim(banks_here, position, 1, keepdims=False)
        return running + jnp.einsum(
            "rij,rjf->rif",
            tile_bank[bank_ids],
            feat_blocks[column],
            preferred_element_type=jnp.float32,
        )

    running = lax.fori_loop(
        0, tiles_row, forward_tiles, jnp.zeros((blocks, tile_size, narrow), jnp.float32)
    )
    shared = feat_blocks[own_pub]
    everyone = lax.all_gather(shared, "dom", axis=0, tiled=True)
    remote = everyone[gathered_ids]
    halo_terms = (
        jnp.einsum("dsij,dsjf->dsif", halo_tiles, remote, preferred_element_type=jnp.float32)
        * live_in
    )
    running = running + jax.ops.segment_sum(
        halo_terms.reshape(domains * slot_count, tile_size, narrow),
        rows_in.reshape(-1),
        num_segments=blocks,
    )
    agg_narrow = running.astype(jnp.bfloat16).reshape(part_rows, narrow)
    aggregated = lax.all_to_all(agg_narrow, "grp", split_axis=0, concat_axis=1, tiled=True)
    pre_act = jnp.dot(aggregated, weight, preferred_element_type=jnp.float32) + bias
    activations = jnp.maximum(pre_act, 0.0).astype(jnp.bfloat16)
    grad_pre = jnp.where(pre_act > 0, cotangent.astype(jnp.float32), 0.0).astype(jnp.bfloat16)
    weight_part = lax.dot_general(
        aggregated, grad_pre, (((0,), (0,)), ((), ())), preferred_element_type=jnp.float32
    )
    bias_part = jnp.sum(grad_pre.astype(jnp.float32), axis=0)
    grad_agg = lax.dot_general(
        grad_pre, weight, (((1,), (1,)), ((), ())), preferred_element_type=jnp.float32
    ).astype(jnp.bfloat16)
    grad_narrow = lax.all_to_all(grad_agg, "grp", split_axis=1, concat_axis=0, tiled=True)
    grad_blocks = grad_narrow.reshape(blocks, tile_size, narrow)

    def backward_tiles(position, running):
        column = lax.dynamic_index_in_dim(cols_here, position, 1, keepdims=False)
        bank_ids = lax.dynamic_index_in_dim(banks_here, position, 1, keepdims=False)
        contrib = jnp.einsum(
            "rji,rjf->rif", tile_bank[bank_ids], grad_blocks, preferred_element_type=jnp.float32
        )
        return running + jax.ops.segment_sum(contrib, column, num_segments=blocks)

    grad_total = lax.fori_loop(
        0, tiles_row, backward_tiles, jnp.zeros((blocks, tile_size, narrow), jnp.float32)
    )
    back_terms = (
        jnp.einsum(
            "dsji,dsjf->dsif", halo_tiles, grad_blocks[rows_in], preferred_element_type=jnp.float32
        )
        * live_in
    )
    placed = jax.ops.segment_sum(
        back_terms.reshape(domains * slot_count, tile_size, narrow),
        gathered_ids.reshape(-1),
        num_segments=domains * pub_count,
    )
    mine_back = lax.psum_scatter(placed, "dom", scatter_dimension=0, tiled=True)
    back_total = jax.ops.segment_sum(mine_back, own_pub, num_segments=blocks)
    grad_total = grad_total + back_total
    grad_nodes = lax.all_to_all(
        grad_total.astype(jnp.bfloat16).reshape(part_rows, narrow),
        "grp",
        split_axis=0,
        concat_axis=1,
        tiled=True,
    )
    norm_scale = float(rows_here * groups * domains) ** (-0.5)
    weight_total, bias_total = lax.psum((weight_part, bias_part), ("dom", "grp"))
    return (activations, grad_nodes, weight_total * norm_scale, bias_total * norm_scale)


def solution(mesh):
    in_specs = (
        P(("dom", "grp"), None),
        P(),
        P(),
        P(("dom", "grp"), None),
        P(),
        P("dom", None, None),
        P("dom", None, None),
        P("dom", None),
        P(),
        P("dom", None, None),
        P("dom", None, None),
    )
    out_specs = (P(("dom", "grp"), None), P(("dom", "grp"), None), P(), P())
    return jax.shard_map(
        per_device, mesh=mesh, in_specs=in_specs, out_specs=out_specs, check_vma=False
    )
```

profile of v0, /device:TPU:2, one launch (start us, length us, event | category | flops | bytes accessed | tf_op | source)
XLA Modules:
  0.0 686.9 jit_solution(15913844381797116386)
XLA Ops:
  9.3 4.5 all-to-all-start
  17.1 7.1 %all-to-all-done = bf16[256,8,128]{2,0,1:T(8,128)(2,1)} async-done(((bf16[256,8,128]{2,0,1:T(8,128)(2,1)}), bf16[256,8,128]{2,0,1:T(8,128)(2,1)}, u32[]{:S(2)}, u32[]{:S(2)}) %all-to-all-start) | async-done | bytes 524320 | tf_op jit(solution)/shard_map/all_to_all | solution.py:28
  26.5 74.0 %while.28 = (s32[]{:T(128)}, f32[16,128,128]{2,1,0:T(8,128)S(1)}, s32[16,16]{0,1:T(8,128)S(1)}, bf16[16,128,128]{2,1,0:T(8,128)(2,1)S(1)}, s32[16,16]{0,1:T(8,12...) while((s32[]{:T(128)}, f32[16,128,128]{2,1,0:T(8,128)S(1)}, ...), condition=%wide.region_1.2_spmd.clone, body=%wide.region_0.1_spmd.clone.sunk | while | flops 67635296 | bytes 5251683 | solution.py:52
  100.5 7.6 %all-gather.3.cloned.1.call-done = bf16[128,128,128]{2,1,0:T(8,128)(2,1)} async-done(((bf16[4,128,128]{2,1,0:T(8,128)(2,1)}), bf16[128,128,128]{2,1,0:T(8,128)(2,1)}) %all-gather.3.cloned.1.call-update) | async-done | bytes 4194320 | tf_op jit(solution)/shard_map/all_gather | solution.py:56
  108.1 4.3 gather_fusion.5
  112.4 4.9 convolution_multiply_fusion.1
  117.2 8.8 %scatter_fusion.1 = f32[16,128,128]{2,1,0:T(8,128)S(1)} fusion(f32[16,128,128]{2,1,0:T(8,128)S(1)} %get-tuple-element.222, s32[64]{0:T(128)S(1)} %reshape.272, f32[64,128,128]{2,1,0:T(8,128)} %bitcast.94), kind=kCustom, calls=%fused_computation.8 | custom fusion | flops 1048576 | bytes 12583168 | tf_op jit(solution)/shard_map/scatter-add | solution.py:62
  126.9 4.4 all-to-all-start.1
  131.6 10.1 %all-to-all-done.1 = bf16[8,256,128]{2,1,0:T(8,128)(2,1)S(1)} async-done(((bf16[8,256,128]{2,1,0:T(8,128)(2,1)}), bf16[8,256,128]{2,1,0:T(8,128)(2,1)S(1)}, u32[]{:S(2)}, u32[]{:S(2)}) %all-to-all-start.1) | async-done | bytes 524320 | tf_op jit(solution)/shard_map/all_to_all | solution.py:68
  144.6 3.5 all-to-all-start.2
  148.6 9.8 %all-to-all-done.2 = bf16[256,8,128]{2,0,1:T(8,128)(2,1)S(1)} async-done(((bf16[256,8,128]{2,0,1:T(8,128)(2,1)}), bf16[256,8,128]{2,0,1:T(8,128)(2,1)S(1)}, u32[]{:S(2)}, u32[]{:S(2)}) %all-to-all-start.2) | async-done | bytes 524320 | tf_op jit(solution)/shard_map/all_to_all | solution.py:79
  160.5 5.2 convolution_multiply_fusion
  165.8 4.3 broadcast_in_dim.12
  170.0 13.4 %scatter_fusion.2 = f32[128,128,128]{2,1,0:T(8,128)} fusion(f32[128,128,128]{2,1,0:T(8,128)} %broadcast_in_dim.12, s32[64]{0:T(128)S(1)} %add_bitcast_fusion, f32[64,128,128]{2,1,0:T(8,128)} %bitcast.93), kind=kCustom, calls=%fused_computation.9 | custom fusion | flops 1048576 | bytes 12583168 | tf_op jit(solution)/shard_map/scatter-add | solution.py:99
  183.5 75.8 %psum.15 = f32[512]{0:T(512)S(1)} all-reduce(f32[512]{0:T(512)S(1)} %get-tuple-element.277), channel_id=1, replica_groups=mesh['dom'=32,'grp'=8] {'dom','grp'}, use_global_device_ids=true, to_apply=%region_11.12 | all-reduce | flops 512 | bytes 4096 | tf_op jit(solution)/shard_map/psum | solution.py:115
  262.2 98.2 %while.27 = (s32[]{:T(128)}, f32[16,128,128]{2,1,0:T(8,128)}, s32[16,16]{0,1:T(8,128)S(1)}, s32[16,16]{0,1:T(8,128)S(1)}, bf16[16,128,128]{2,1,0:T(8,128)(2,1)S(...) while((s32[]{:T(128)}, f32[16,128,128]{2,1,0:T(8,128)}, s32[16,16]{0,1:T(8,128)S(1)}, ...), condition=%wide.region_5.6_spmd, body=%wide.region_3.5_spmd.sunk | while | flops 67372080 | bytes 6296081 | solution.py:90
  265.0 3.3 scatter_fusion
  283.4 3.3 scatter_fusion
  289.6 3.3 scatter_fusion
  301.9 3.3 scatter_fusion
  320.3 3.4 scatter_fusion
  360.4 48.2 %reduce-scatter.2.cloned.1.call-done = f32[4,128,128]{2,1,0:T(8,128)} async-done(((f32[128,128,128]{2,1,0:T(8,128)}), f32[4,128,128]{2,1,0:T(8,128)}) %reduce-scatter.2.cloned.1.call-update) | async-done | bytes 262160 | tf_op jit(solution)/shard_map/reduce_scatter | solution.py:104
  413.3 4.3 all-to-all-start.3
  418.1 257.9 %all-reduce.2.cloned.1.call-done = f32[1024,512]{1,0:T(8,128)} async-done(((f32[1024,512]{1,0:T(8,128)}), f32[1024,512]{1,0:T(8,128)}) %all-reduce.2.cloned.1.call-update) | async-done | bytes 2097168 | tf_op jit(solution)/shard_map/psum | solution.py:115
  (246 shorter events, 181.0 us)
Async XLA Ops:
  7.2 134.8 %copy-start = (bf16[1024,512]{1,0:T(8,128)(2,1)S(1)}, bf16[1024,512]{1,0:T(8,128)(2,1)}, u32[]{:S(2)}) copy-start(bf16[1024,512]{1,0:T(8,128)(2,1)} %param.16) | copy-start | bytes 3145732
  7.2 6.6 copy-start.3
  7.2 6.8 copy-start.8
  7.2 7.4 %copy-start.4 = (s32[1,16,16]{2,1,0:T(8,128)S(1)}, s32[1,16,16]{2,1,0:T(8,128)}, u32[]{:S(2)}) copy-start(s32[1,16,16]{2,1,0:T(8,128)} %param.21) | copy-start | bytes 3076
  7.2 7.4 %copy-start.5 = (s32[1,16,16]{2,1,0:T(8,128)S(1)}, s32[1,16,16]{2,1,0:T(8,128)}, u32[]{:S(2)}) copy-start(s32[1,16,16]{2,1,0:T(8,128)} %param.20) | copy-start | bytes 3076
  7.2 7.5 %copy-start.6 = (s32[1,32,2]{1,2,0:T(2,128)S(1)}, s32[1,32,2]{1,2,0:T(2,128)}, u32[]{:S(2)}) copy-start(s32[1,32,2]{1,2,0:T(2,128)} %param.24) | copy-start | bytes 772
  7.2 7.7 %copy-start.1 = (bf16[16,128,128]{2,1,0:T(8,128)(2,1)S(1)}, bf16[16,128,128]{2,1,0:T(8,128)(2,1)}, u32[]{:S(2)}) copy-start(bf16[16,128,128]{2,1,0:T(8,128)(2,1)} %param.19) | copy-start | bytes 1572868
  9.3 14.9 %all-to-all-start = ((bf16[256,8,128]{2,0,1:T(8,128)(2,1)}), bf16[256,8,128]{2,0,1:T(8,128)(2,1)}, u32[]{:S(2)}, u32[]{:S(2)}) async-start(bf16[256,8,128]{2,0,1:T(8,128)(2,1)} %copy_bitcast_fusion.1), calls=%async_computation | async-start | bytes 1048576 | tf_op jit(solution)/shard_map/all_to_all | solution.py:28
  13.8 94.3 %all-gather.3.cloned.1.call-start = ((), (), s32[]{:S(2)}) async-start(), calls=%async_computation.7 | async-start | bytes 4325376 | tf_op jit(solution)/shard_map/all_gather | solution.py:56
  14.9 2.2 copy-start.9
  126.0 15.9 %copy-start.7 = (f32[512]{0:T(512)S(1)}, f32[512]{0:T(512)}, u32[]{:S(2)}) copy-start(f32[512]{0:T(512)} %param.17) | copy-start | bytes 6148
  126.9 16.2 %copy-start.2 = (bf16[256,512]{1,0:T(8,128)(2,1)S(1)}, bf16[256,512]{1,0:T(8,128)(2,1)}, u32[]{:S(2)}) copy-start(bf16[256,512]{1,0:T(8,128)(2,1)} %param.18) | copy-start | bytes 786436
  126.9 14.8 %all-to-all-start.1 = ((bf16[8,256,128]{2,1,0:T(8,128)(2,1)}), bf16[8,256,128]{2,1,0:T(8,128)(2,1)S(1)}, u32[]{:S(2)}, u32[]{:S(2)}) async-start(bf16[8,256,128]{2,1,0:T(8,128)(2,1)} %bitcast.15), calls=%async_computation.1 | async-start | bytes 1048576 | tf_op jit(solution)/shard_map/all_to_all | solution.py:68
  144.6 13.8 %all-to-all-start.2 = ((bf16[256,8,128]{2,0,1:T(8,128)(2,1)}), bf16[256,8,128]{2,0,1:T(8,128)(2,1)S(1)}, u32[]{:S(2)}, u32[]{:S(2)}) async-start(bf16[256,8,128]{2,0,1:T(8,128)(2,1)} %bitcast.76), calls=%async_computation.2 | async-start | bytes 1048576 | tf_op jit(solution)/shard_map/all_to_all | solution.py:79
  148.1 260.6 %reduce-scatter.2.cloned.1.call-start = ((), (), s32[]{:S(2)}) async-start(), calls=%async_computation.5 | async-start | bytes 8650752 | tf_op jit(solution)/shard_map/reduce_scatter | solution.py:104
  183.5 492.5 %all-reduce.2.cloned.1.call-start = ((), (), s32[]{:S(2)}) async-start(), calls=%async_computation.6 | async-start | bytes 4194304 | tf_op jit(solution)/shard_map/psum | solution.py:115
  413.3 265.9 %all-to-all-start.3 = ((bf16[8,256,128]{2,1,0:T(8,128)(2,1)}), bf16[8,256,128]{2,1,0:T(8,128)(2,1)S(1)}, u32[]{:S(2)}, u32[]{:S(2)}) async-start(bf16[8,256,128]{2,1,0:T(8,128)(2,1)} %bitcast.26), calls=%async_computation.4 | async-start | bytes 1048576 | tf_op jit(solution)/shard_map/all_to_all | solution.py:107
Sparse Core Ops, SparseCore 0:
  26.6 81.3 all-gather.2
  183.6 225.0 reduce-scatter.1
  415.5 260.4 all-reduce.1
where the time goes:
time: 691 us; the launch traced here: 687 us
  waiting for transfers between devices  341 us (49%)
  local copies, waits for them, and re-layouts  94.3 us (14%)
  other arithmetic  85.3 us (12%)
  blocking collectives  75.8 us (11%)
  matrix products  58.9 us (9%)
  starting transfers between devices  16.8 us (2%)
  between operations  14 us (2%)
    psum x1, waiting for transfers between devices, per_device(): lax.psum((weight_part, bias_part), ('dom', 'grp'))  258 us
    psum x1, blocking collectives, per_device(): lax.psum((weight_part, bias_part), ('dom', 'grp'))  75.8 us
    scatter-add x16, other arithmetic, backward_tiles(): return running + jax.ops.segment_sum(contrib, column, num_segments=blocks)  53.1 us
    reduce_scatter x1, waiting for transfers between devices, per_device(): mine_back = lax.psum_scatter(placed, 'dom', scatter_dimension=0, tiled=True)  48.2 us
    gather x16, local copies, waits for them, and re-layouts, forward_tiles(): feat_blocks[column]  39.2 us
    dot_general x16, matrix products, forward_tiles(): jnp.einsum('rij,rjf->rif', tile_bank[bank_ids], feat_blocks[column], pref...  23.2 us
    gather x16, local copies, waits for them, and re-layouts, backward_tiles(): tile_bank[bank_ids]  22.5 us
    dot_general x16, matrix products, backward_tiles(): jnp.einsum('rji,rjf->rif', tile_bank[bank_ids], grad_blocks, preferred_el...  22.3 us
  transfers between devices with their start and end apart: 7, of which 6 were waited for; matrix products, arithmetic and copies ran while one was open for 27% of the time, Pallas kernels for 0%

commit v1 on v0

--- a/solution.py
+++ b/solution.py
@@ -112,7 +112,7 @@
         tiled=True,
     )
     norm_scale = float(rows_here * groups * domains) ** (-0.5)
-    weight_total, bias_total = lax.psum((weight_part, bias_part), ("dom", "grp"))
+    weight_total, bias_total = lax.psum(lax.psum((weight_part, bias_part), "grp"), "dom")
     return (activations, grad_nodes, weight_total * norm_scale, bias_total * norm_scale)
 
 

time: 691 us -> 619 us (0.90)
  waiting for transfers between devices: 341 us -> 266 us
    psum x1 -> x2, waiting for transfers between devices: 258 us -> 146 us  [the longest x1 146 us: per_device(): lax.psum(lax.psum((weight_part, bias_part), 'grp'), 'dom')]
    reduce_scatter x1, waiting for transfers between devices: 48.2 us -> 82.5 us  [per_device(): mine_back = lax.psum_scatter(placed, 'dom', scatter_dimension=0, tiled=True)]
    psum x1 -> x2, blocking collectives: 75.8 us -> 76.6 us  [the longest x1 64.2 us: per_device(): lax.psum(lax.psum((weight_part, bias_part), 'grp'), 'dom')]
  transfers between devices with their start and end apart: 7 -> 8, of which waited for: 6 -> 6; matrix products, arithmetic and copies ran while one was open for 27% -> 34% of each run, Pallas kernels for 0% -> 0%
where the time goes in v1:
time: 619 us; the launch traced here: 613 us
  waiting for transfers between devices  266 us (43%)
  local copies, waits for them, and re-layouts  94.3 us (15%)
  other arithmetic  85 us (14%)
  blocking collectives  76.6 us (12%)
  matrix products  59 us (10%)
  starting transfers between devices  16.8 us (3%)
  between operations  14.1 us (2%)
    psum x1, waiting for transfers between devices, per_device(): lax.psum(lax.psum((weight_part, bias_part), 'grp'), 'dom')  146 us
    reduce_scatter x1, waiting for transfers between devices, per_device(): mine_back = lax.psum_scatter(placed, 'dom', scatter_dimension=0, tiled=True)  82.5 us
    psum x1, blocking collectives, per_device(): lax.psum(lax.psum((weight_part, bias_part), 'grp'), 'dom')  64.2 us
    scatter-add x16, other arithmetic, backward_tiles(): return running + jax.ops.segment_sum(contrib, column, num_segments=blocks)  52.7 us
    gather x16, local copies, waits for them, and re-layouts, forward_tiles(): feat_blocks[column]  39.2 us
    dot_general x16, matrix products, forward_tiles(): jnp.einsum('rij,rjf->rif', tile_bank[bank_ids], feat_blocks[column], pref...  23.2 us
    gather x16, local copies, waits for them, and re-layouts, backward_tiles(): tile_bank[bank_ids]  22.5 us
    dot_general x16, matrix products, backward_tiles(): jnp.einsum('rji,rjf->rif', tile_bank[bank_ids], grad_blocks, preferred_el...  22.3 us
  transfers between devices with their start and end apart: 8, of which 6 were waited for; matrix products, arithmetic and copies ran while one was open for 34% of the time, Pallas kernels for 0%

profile of v1, /device:TPU:2, one launch (start us, length us, event | category | flops | bytes accessed | tf_op | source)
XLA Modules:
  0.0 612.8 jit_solution(13723840130877522859)
XLA Ops:
  9.3 4.5 all-to-all-start
  17.1 7.1 %all-to-all-done = bf16[256,8,128]{2,0,1:T(8,128)(2,1)} async-done(((bf16[256,8,128]{2,0,1:T(8,128)(2,1)}), bf16[256,8,128]{2,0,1:T(8,128)(2,1)}, u32[]{:S(2)}, u32[]{:S(2)}) %all-to-all-start) | async-done | bytes 524320 | tf_op jit(solution)/shard_map/all_to_all | solution.py:28
  26.5 74.0 %while.28 = (s32[]{:T(128)}, f32[16,128,128]{2,1,0:T(8,128)S(1)}, s32[16,16]{0,1:T(8,128)S(1)}, bf16[16,128,128]{2,1,0:T(8,128)(2,1)S(1)}, s32[16,16]{0,1:T(8,12...) while((s32[]{:T(128)}, f32[16,128,128]{2,1,0:T(8,128)S(1)}, ...), condition=%wide.region_1.2_spmd.clone, body=%wide.region_0.1_spmd.clone.sunk | while | flops 67635296 | bytes 5251683 | solution.py:52
  100.5 7.6 %all-gather.3.cloned.1.call-done = bf16[128,128,128]{2,1,0:T(8,128)(2,1)} async-done(((bf16[4,128,128]{2,1,0:T(8,128)(2,1)}), bf16[128,128,128]{2,1,0:T(8,128)(2,1)}) %all-gather.3.cloned.1.call-update) | async-done | bytes 4194320 | tf_op jit(solution)/shard_map/all_gather | solution.py:56
  108.1 4.3 gather_fusion.5
  112.4 4.9 convolution_multiply_fusion.1
  117.2 8.8 %scatter_fusion.1 = f32[16,128,128]{2,1,0:T(8,128)S(1)} fusion(f32[16,128,128]{2,1,0:T(8,128)S(1)} %get-tuple-element.222, s32[64]{0:T(128)S(1)} %reshape.272, f32[64,128,128]{2,1,0:T(8,128)} %bitcast.94), kind=kCustom, calls=%fused_computation.8 | custom fusion | flops 1048576 | bytes 12583168 | tf_op jit(solution)/shard_map/scatter-add | solution.py:62
  126.9 4.4 all-to-all-start.1
  131.6 10.1 %all-to-all-done.1 = bf16[8,256,128]{2,1,0:T(8,128)(2,1)S(1)} async-done(((bf16[8,256,128]{2,1,0:T(8,128)(2,1)}), bf16[8,256,128]{2,1,0:T(8,128)(2,1)S(1)}, u32[]{:S(2)}, u32[]{:S(2)}) %all-to-all-start.1) | async-done | bytes 524320 | tf_op jit(solution)/shard_map/all_to_all | solution.py:68
  146.4 3.5 all-to-all-start.2
  150.3 12.3 %all-to-all-done.2 = bf16[256,8,128]{2,0,1:T(8,128)(2,1)S(1)} async-done(((bf16[256,8,128]{2,0,1:T(8,128)(2,1)}), bf16[256,8,128]{2,0,1:T(8,128)(2,1)S(1)}, u32[]{:S(2)}, u32[]{:S(2)}) %all-to-all-start.2) | async-done | bytes 524320 | tf_op jit(solution)/shard_map/all_to_all | solution.py:79
  164.8 5.3 convolution_multiply_fusion
  170.1 4.3 broadcast_in_dim.12
  174.3 13.5 %scatter_fusion.2 = f32[128,128,128]{2,1,0:T(8,128)} fusion(f32[128,128,128]{2,1,0:T(8,128)} %broadcast_in_dim.12, s32[64]{0:T(128)S(1)} %add_bitcast_fusion, f32[64,128,128]{2,1,0:T(8,128)} %bitcast.93), kind=kCustom, calls=%fused_computation.9 | custom fusion | flops 1048576 | bytes 12583168 | tf_op jit(solution)/shard_map/scatter-add | solution.py:99
  187.9 12.5 %psum.30 = f32[512]{0:T(512)S(1)} all-reduce(f32[512]{0:T(512)S(1)} %get-tuple-element.277), channel_id=1, replica_groups=mesh['dom'=32,'grp'=8] {'grp'}, use_global_device_ids=true, to_apply=%region_12.13 | all-reduce | flops 512 | bytes 4096 | tf_op jit(solution)/shard_map/psum | solution.py:115
  200.4 64.2 %psum.31 = f32[512]{0:T(512)S(1)} all-reduce(f32[512]{0:T(512)S(1)} %psum.30), channel_id=1, replica_groups=mesh['dom'=32,'grp'=8] {'dom'}, use_global_device_ids=true, to_apply=%region_13.14 | all-reduce | flops 512 | bytes 4096 | tf_op jit(solution)/shard_map/psum | solution.py:115
  265.7 97.9 %while.27 = (s32[]{:T(128)}, f32[16,128,128]{2,1,0:T(8,128)}, s32[16,16]{0,1:T(8,128)S(1)}, s32[16,16]{0,1:T(8,128)S(1)}, bf16[16,128,128]{2,1,0:T(8,128)(2,1)S(...) while((s32[]{:T(128)}, f32[16,128,128]{2,1,0:T(8,128)}, s32[16,16]{0,1:T(8,128)S(1)}, ...), condition=%wide.region_5.6_spmd, body=%wide.region_3.5_spmd.sunk | while | flops 67372080 | bytes 6296081 | solution.py:90
  268.5 3.3 scatter_fusion
  293.0 3.3 scatter_fusion
  311.4 3.3 scatter_fusion
  323.6 3.3 scatter_fusion
  363.6 82.5 %reduce-scatter.2.cloned.1.call-done = f32[4,128,128]{2,1,0:T(8,128)} async-done(((f32[128,128,128]{2,1,0:T(8,128)}), f32[4,128,128]{2,1,0:T(8,128)}) %reduce-scatter.2.cloned.1.call-update) | async-done | bytes 262160 | tf_op jit(solution)/shard_map/reduce_scatter | solution.py:104
  450.7 4.3 all-to-all-start.3
  455.6 146.3 %all-reduce.5.cloned.1.call-done = f32[1024,512]{1,0:T(8,128)} async-done(((f32[1024,512]{1,0:T(8,128)}), f32[1024,512]{1,0:T(8,128)}) %all-reduce.5.cloned.1.call-update) | async-done | bytes 2097168 | tf_op jit(solution)/shard_map/psum | solution.py:115
  (250 shorter events, 184.1 us)
Async XLA Ops:
  7.2 134.8 %copy-start = (bf16[1024,512]{1,0:T(8,128)(2,1)S(1)}, bf16[1024,512]{1,0:T(8,128)(2,1)}, u32[]{:S(2)}) copy-start(bf16[1024,512]{1,0:T(8,128)(2,1)} %param.16) | copy-start | bytes 3145732
  7.2 6.6 %copy-start.3 = (s32[32,32,2]{1,2,0:T(2,128)S(1)}, s32[32,32,2]{1,2,0:T(2,128)}, u32[]{:S(2)}) copy-start(s32[32,32,2]{1,2,0:T(2,128)} %param.23) | copy-start | bytes 24580
  7.2 6.8 %copy-start.8 = (s32[1,32,2]{1,2,0:T(2,128)S(1)}, s32[1,32,2]{1,2,0:T(2,128)}, u32[]{:S(2)}) copy-start(s32[1,32,2]{1,2,0:T(2,128)} %param.25) | copy-start | bytes 772
  7.2 7.4 %copy-start.4 = (s32[1,16,16]{2,1,0:T(8,128)S(1)}, s32[1,16,16]{2,1,0:T(8,128)}, u32[]{:S(2)}) copy-start(s32[1,16,16]{2,1,0:T(8,128)} %param.21) | copy-start | bytes 3076
  7.2 7.4 %copy-start.5 = (s32[1,16,16]{2,1,0:T(8,128)S(1)}, s32[1,16,16]{2,1,0:T(8,128)}, u32[]{:S(2)}) copy-start(s32[1,16,16]{2,1,0:T(8,128)} %param.20) | copy-start | bytes 3076
  7.2 7.5 %copy-start.6 = (s32[1,32,2]{1,2,0:T(2,128)S(1)}, s32[1,32,2]{1,2,0:T(2,128)}, u32[]{:S(2)}) copy-start(s32[1,32,2]{1,2,0:T(2,128)} %param.24) | copy-start | bytes 772
  7.2 7.7 %copy-start.1 = (bf16[16,128,128]{2,1,0:T(8,128)(2,1)S(1)}, bf16[16,128,128]{2,1,0:T(8,128)(2,1)}, u32[]{:S(2)}) copy-start(bf16[16,128,128]{2,1,0:T(8,128)(2,1)} %param.19) | copy-start | bytes 1572868
  9.3 14.9 %all-to-all-start = ((bf16[256,8,128]{2,0,1:T(8,128)(2,1)}), bf16[256,8,128]{2,0,1:T(8,128)(2,1)}, u32[]{:S(2)}, u32[]{:S(2)}) async-start(bf16[256,8,128]{2,0,1:T(8,128)(2,1)} %copy_bitcast_fusion.1), calls=%async_computation | async-start | bytes 1048576 | tf_op jit(solution)/shard_map/all_to_all | solution.py:28
  13.8 94.3 %all-gather.3.cloned.1.call-start = ((), (), s32[]{:S(2)}) async-start(), calls=%async_computation.8 | async-start | bytes 4325376 | tf_op jit(solution)/shard_map/all_gather | solution.py:56
  14.9 2.2 copy-start.9
  126.0 15.9 %copy-start.7 = (f32[512]{0:T(512)S(1)}, f32[512]{0:T(512)}, u32[]{:S(2)}) copy-start(f32[512]{0:T(512)} %param.17) | copy-start | bytes 6148
  126.9 16.2 %copy-start.2 = (bf16[256,512]{1,0:T(8,128)(2,1)S(1)}, bf16[256,512]{1,0:T(8,128)(2,1)}, u32[]{:S(2)}) copy-start(bf16[256,512]{1,0:T(8,128)(2,1)} %param.18) | copy-start | bytes 786436
  126.9 14.8 %all-to-all-start.1 = ((bf16[8,256,128]{2,1,0:T(8,128)(2,1)}), bf16[8,256,128]{2,1,0:T(8,128)(2,1)S(1)}, u32[]{:S(2)}, u32[]{:S(2)}) async-start(bf16[8,256,128]{2,1,0:T(8,128)(2,1)} %bitcast.15), calls=%async_computation.1 | async-start | bytes 1048576 | tf_op jit(solution)/shard_map/all_to_all | solution.py:68
  131.4 133.2 %all-reduce.3.cloned.1.call-start = ((), (), s32[]{:S(2)}) async-start(), calls=%async_computation.6 | async-start | bytes 4194304 | tf_op jit(solution)/shard_map/psum | solution.py:115
  146.4 16.2 %all-to-all-start.2 = ((bf16[256,8,128]{2,0,1:T(8,128)(2,1)}), bf16[256,8,128]{2,0,1:T(8,128)(2,1)S(1)}, u32[]{:S(2)}, u32[]{:S(2)}) async-start(bf16[256,8,128]{2,0,1:T(8,128)(2,1)} %bitcast.76), calls=%async_computation.2 | async-start | bytes 1048576 | tf_op jit(solution)/shard_map/all_to_all | solution.py:79
  149.9 296.2 %reduce-scatter.2.cloned.1.call-start = ((), (), s32[]{:S(2)}) async-start(), calls=%async_computation.5 | async-start | bytes 8650752 | tf_op jit(solution)/shard_map/reduce_scatter | solution.py:104
  187.9 414.0 %all-reduce.5.cloned.1.call-start = ((), (), s32[]{:S(2)}) async-start(), calls=%async_computation.7 | async-start | bytes 4194304 | tf_op jit(solution)/shard_map/psum | solution.py:115
  450.7 154.4 %all-to-all-start.3 = ((bf16[8,256,128]{2,1,0:T(8,128)(2,1)}), bf16[8,256,128]{2,1,0:T(8,128)(2,1)S(1)}, u32[]{:S(2)}, u32[]{:S(2)}) async-start(bf16[8,256,128]{2,1,0:T(8,128)(2,1)} %bitcast.26), calls=%async_computation.4 | async-start | bytes 1048576 | tf_op jit(solution)/shard_map/all_to_all | solution.py:107
Sparse Core Ops, SparseCore 0:
  26.6 81.3 all-gather.2
  145.1 69.2 all-reduce.2
  218.5 227.5 reduce-scatter.1
  449.9 151.9 all-reduce.4
